TPU v7x, 32 devices: a whole 2x2x4 slice. The times are simulated.
32 devices in a mesh: wide: 8 (over y, x, core), narrow: 4 (over z).
Axes of the slice: x: 2, y: 2, z: 4, core: 2. Of those that a mesh axis runs over, the one named last changes fastest.
Arguments:
- amps: float32 [1, 16, 640, 640], P(None, 'wide', 'narrow'), may hold values from -6 to 6
- cycle: float32 [16, 640, 5120], P(None, 'wide', 'narrow'), may hold values from -0.25 to 0.25
- irrep_i: int32 [1], replicated, may hold values from 0 to 7
- irrep_k: int32 [16], replicated, may hold values from 0 to 7, as said below
- irrep_j: int32 [8], replicated, may hold values from 0 to 7, as said below
- irrep_v: int32 [640], replicated, may hold values from 0 to 7, as said below
Outputs:
- cycle_term: float32 [1, 8, 640, 640], P(None, 'wide', 'narrow')
Inputs may be any that keep to these rules, and one draw needn't show every extreme that they name: `irrep_k`: nondecreasing along the orbitals, the first 0 and the last 7. `irrep_j`: nondecreasing along the orbitals, the first 0 and the last 7. `irrep_v`: nondecreasing along the orbitals, the first 0 and the last 7.
All inputs are finite; a program needn't handle non-finite values.
Results may differ from a plain program's by a relative error of at most 0.000071.
Values sent between devices are 32-bit elements; how exact they have to be, the bound alone decides.
A program may use at most 64 MiB of HBM per device.

v0:
```python
import jax
import jax.numpy as jnp
from jax import lax
from jax.sharding import PartitionSpec as P


def per_device(amps, cycle, irrep_i, irrep_k, irrep_j, irrep_v):
    wide_pos = lax.axis_index("wide")
    narrow_pos = lax.axis_index("narrow")
    wide_count = lax.axis_size("wide")
    narrow_count = lax.axis_size("narrow")
    i_total = amps.shape[0]
    k_local = amps.shape[1]
    a_local = amps.shape[2]
    v_total = amps.shape[3]
    k_total = cycle.shape[0]
    c_local = cycle.shape[1]
    b_local = v_total // narrow_count
    j_total = cycle.shape[2] // b_local
    j_local = j_total // wide_count
    cycle_four = cycle.reshape(k_total, c_local, b_local, j_total)
    k_labels = lax.dynamic_slice_in_dim(irrep_k, wide_pos * k_local, k_local)
    a_labels = lax.dynamic_slice_in_dim(irrep_v, narrow_pos * a_local, a_local)
    allowed_in = (
        irrep_i[:, None, None, None]
        ^ k_labels[None, :, None, None]
        ^ a_labels[None, None, :, None]
        ^ irrep_v[None, None, None, :]
        == 0
    )
    masked = jnp.where(allowed_in, amps, jnp.zeros_like(amps))
    moved = lax.all_to_all(masked, "wide", split_axis=3, concat_axis=1, tiled=True)
    piece = lax.all_gather(moved, "narrow", axis=2, tiled=True)
    part_sum = jnp.einsum("ikac,kcbj->iajb", piece, cycle_four, precision=lax.Precision.HIGHEST)
    terms = part_sum.reshape(piece.shape[0], piece.shape[2], j_total * b_local)
    summed = lax.psum_scatter(terms, "wide", scatter_dimension=2, tiled=True)
    summed_four = summed.reshape(i_total, v_total, j_local, b_local)
    j_labels = lax.dynamic_slice_in_dim(irrep_j, wide_pos * j_local, j_local)
    b_labels = lax.dynamic_slice_in_dim(irrep_v, narrow_pos * b_local, b_local)
    allowed_out = (
        irrep_i[:, None, None, None]
        ^ irrep_v[None, :, None, None]
        ^ j_labels[None, None, :, None]
        ^ b_labels[None, None, None, :]
        == 0
    )
    result = jnp.where(allowed_out, summed_four, jnp.zeros_like(summed_four)).reshape(
        i_total, v_total, j_local * b_local
    )
    returned = lax.all_to_all(result, "narrow", split_axis=1, concat_axis=2, tiled=True)
    spread = returned.reshape(i_total, a_local, narrow_count, j_local, b_local)
    return jnp.transpose(spread, (0, 3, 1, 2, 4)).reshape(i_total, j_local, a_local, v_total)


def solution(mesh):
    placed = (P(None, "wide", "narrow", None), P(None, "wide", "narrow"), P(), P(), P(), P())
    return jax.shard_map(
        per_device,
        mesh=mesh,
        in_specs=placed,
        out_specs=P(None, "wide", "narrow", None),
        check_vma=False,
    )
```

profile of v0, /device:TPU:0, one launch (start us, length us, event | category | flops | bytes accessed | tf_op | source)
XLA Modules:
  0.0 275.7 jit_solution(13251704546821410816)
XLA Ops:
  6.5 0.0 all-gather.2.cloned.1.call-start
  7.2 2.5 copy.21
  9.7 0.8 dynamic_slice.11
  10.5 0.7 dynamic-slice_xor_fusion
  11.2 0.1 broadcast_xor_fusion
  11.3 2.5 compare_select_fusion
  13.8 23.1 %all_to_all.33 = f32[1,2,160,640]{2,1,0,3:T(2,128)S(1)} all-to-all(f32[1,2,160,640]{2,1,0,3:T(2,128)S(1)} %compare_select_fusion), channel_id=1, replica_groups=mesh['wide'=8,'narrow'=4] {'wide'}, dimensions={3} | all-to-all | bytes 1638400 | tf_op jit(solution)/shard_map/all_to_all | solution.py:32
  36.9 2.2 copy.22
  39.0 0.0 all-gather.2.cloned.1.call-update
  39.1 0.0 all-reduce.3.cloned.1.call-start
  39.1 9.9 %copy.24 = f32[16,80,1280]{1,2,0:T(8,128)} copy(f32[16,80,1280]{2,1,0:T(8,128)} %param.7) | data formatting | bytes 13107200 | tf_op args[1]
  49.1 87.6 %all-gather.2.cloned.1.call-done = f32[1,16,640,80]{3,1,0,2:T(8,128)} async-done(((f32[1,16,160,80]{3,1,0,2:T(8,128)}), f32[1,16,640,80]{3,1,0,2:T(8,128)}) %all-gather.2.cloned.1.call-update) | async-done | bytes 3276816 | tf_op jit(solution)/shard_map/all_gather | solution.py:33
  136.7 4.5 %copy.23 = f32[1,16,640,80]{2,3,1,0:T(8,128)S(1)} copy(f32[1,16,640,80]{3,1,0,2:T(8,128)} %all-gather.2.cloned.1.call-done) | data formatting | bytes 6553600 | tf_op jit(solution)/shard_map/all_gather | solution.py:33
  141.1 23.5 %fusion = f32[640,160,8,1]{0,1,3,2:T(8,128)S(1)} fusion(f32[16,80,160,8]{1,3,2,0:T(8,128)} %bitcast.27, f32[1,16,640,80]{2,3,1,0:T(8,128)S(1)} %copy.23), kind=kOutput, calls=%fused_computation | convolution fusion | flops 12582912000 | bytes 13107200 | tf_op jit(solution)/shard_map/ikac,kcbj->iajb/dot_general | solution.py:34
  164.6 8.5 %copy.26 = f32[1,640,1280]{1,0,2:T(1,128)} copy(f32[1,640,1280]{1,2,0:T(8,128)S(1)} %bitcast.30) | data formatting | bytes 6553600 | tf_op jit(solution)/shard_map/reshape | solution.py:35
  173.1 0.0 copy-start.1
  173.1 0.0 copy-start.2
  173.1 0.0 copy-start
  173.1 0.0 all-reduce.3.cloned.1.call-update
  173.1 0.6 copy-done.1
  173.8 0.7 dynamic_slice.10
  174.4 0.0 copy-done.2
  174.4 0.7 dynamic-slice
  175.8 0.0 copy-done
  175.8 0.7 xor_xor_fusion
  176.5 66.1 %all-reduce.3.cloned.1.call-done = f32[1,640,1280]{1,0,2:T(1,128)} async-done(((f32[1,640,1280]{1,0,2:T(1,128)}), f32[1,640,1280]{1,0,2:T(1,128)}) %all-reduce.3.cloned.1.call-update) | async-done | bytes 3276816
  242.6 1.5 compare_select_fusion.1
  244.1 1.8 copy.27
  245.8 21.5 %all_to_all.34 = f32[1,640,160]{2,0,1:T(1,128)S(1)} all-to-all(f32[1,640,160]{2,0,1:T(1,128)S(1)} %copy.27), channel_id=1, replica_groups=mesh['wide'=8,'narrow'=4] {'narrow'}, dimensions={1} | all-to-all | bytes 819200 | tf_op jit(solution)/shard_map/all_to_all | solution.py:50
  267.3 0.4 copy.28
  267.8 1.1 reshape_transpose_reshape.3
Async XLA Ops:
  6.5 130.1 %all-gather.2.cloned.1.call-start = ((), (), s32[]{:S(2)}) async-start(), calls=%async_computation.2 | async-start | bytes 6553600 | tf_op jit(solution)/shard_map/all_gather | solution.py:33
  39.1 203.5 %all-reduce.3.cloned.1.call-start = ((), (), s32[]{:S(2)}) async-start(), calls=%async_computation.3 | async-start | bytes 6553600
  173.1 0.7 copy-start.1
  173.1 1.3 copy-start.2
  173.1 2.7 copy-start
Sparse Core Ops, SparseCore 0:
  39.2 97.4 all-gather.1
  173.3 69.2 all-reduce.2
where the time goes:
time: 276 us
  waiting for transfers between devices  154 us (56%)
  blocking collectives  44.7 us (16%)
  local copies, waits for them, and re-layouts  33.6 us (12%)
  matrix products  23.5 us (9%)
  between operations  14.8 us (5%)
  other arithmetic  5.46 us (2%)
    all_gather x1, waiting for transfers between devices, per_device(): piece = lax.all_gather(moved, 'narrow', axis=2, tiled=True)  87.6 us
    unnamed x3, waiting for transfers between devices  66.1 us
    dot_general x1, matrix products, per_device(): jnp.einsum('ikac,kcbj->iajb', piece, cycle_four, precision=lax.Precision....  23.5 us
    all_to_all x1, blocking collectives, per_device(): lax.all_to_all(masked, 'wide', split_axis=3, concat_axis=1, tiled=True)  23.1 us
    all_to_all x1, blocking collectives, per_device(): lax.all_to_all(result, 'narrow', split_axis=1, concat_axis=2, tiled=True)  21.5 us
    unnamed x9, local copies, waits for them, and re-layouts  13.7 us
    reshape x1, local copies, waits for them, and re-layouts, per_device(): terms = part_sum.reshape(piece.shape[0], piece.shape[2], j_total * b_local)  8.52 us
  transfers between devices with their start and end apart: 2, of which 2 were waited for; matrix products, arithmetic and copies ran while one was open for 4% of the time, Pallas kernels for 0%

commit v1 on v0

--- a/solution.py
+++ b/solution.py
@@ -2,6 +2,13 @@
 import jax.numpy as jnp
 from jax import lax
 from jax.sharding import PartitionSpec as P
+
+
+def exchange_blocks(value, axis, split, join):
+    devices = lax.axis_size(axis)
+    pieces = jnp.stack(jnp.split(value, devices, axis=split), axis=0)
+    pieces = lax.all_to_all(pieces, axis, split_axis=0, concat_axis=0)
+    return jnp.concatenate(pieces, axis=join)
 
 
 def per_device(amps, cycle, irrep_i, irrep_k, irrep_j, irrep_v):
@@ -47,7 +54,7 @@
     result = jnp.where(allowed_out, summed_four, jnp.zeros_like(summed_four)).reshape(
         i_total, v_total, j_local * b_local
     )
-    returned = lax.all_to_all(result, "narrow", split_axis=1, concat_axis=2, tiled=True)
+    returned = exchange_blocks(result, "narrow", 1, 2)
     spread = returned.reshape(i_total, a_local, narrow_count, j_local, b_local)
     return jnp.transpose(spread, (0, 3, 1, 2, 4)).reshape(i_total, j_local, a_local, v_total)
 

time: 276 us -> 242 us (0.88)
  waiting for transfers between devices: 154 us -> 131 us
  local copies, waits for them, and re-layouts: 33.6 us -> 22.3 us
    unnamed x3 -> x2, waiting for transfers between devices: 66.1 us -> 0.03 us
    reduce_scatter x0 -> x1, waiting for transfers between devices: none -> 43.4 us  [per_device(): summed = lax.psum_scatter(terms, 'wide', scatter_dimension=2, tiled=True)]
    reshape x1 -> x0, local copies, waits for them, and re-layouts: 8.52 us -> none  [per_device(): terms = part_sum.reshape(piece.shape[0], piece.shape[2], j_total * b_local)]
    unnamed x9 -> x6, local copies, waits for them, and re-layouts: 13.7 us -> 13.1 us
  transfers between devices with their start and end apart: 2 -> 2, of which waited for: 2 -> 2; matrix products, arithmetic and copies ran while one was open for 4% -> 5% of each run, Pallas kernels for 0% -> 0%
where the time goes in v1:
time: 242 us; the launch traced here: 241 us
  waiting for transfers between devices  131 us (54%)
  blocking collectives  44.8 us (19%)
  matrix products  23.8 us (10%)
  local copies, waits for them, and re-layouts  22.3 us (9%)
  between operations  14.1 us (6%)
  other arithmetic  5.13 us (2%)
    all_gather x1, waiting for transfers between devices, per_device(): piece = lax.all_gather(moved, 'narrow', axis=2, tiled=True)  87.6 us
    reduce_scatter x1, waiting for transfers between devices, per_device(): summed = lax.psum_scatter(terms, 'wide', scatter_dimension=2, tiled=True)  43.4 us
    dot_general x1, matrix products, per_device(): jnp.einsum('ikac,kcbj->iajb', piece, cycle_four, precision=lax.Precision....  23.8 us
    all_to_all x1, blocking collectives, per_device(): lax.all_to_all(masked, 'wide', split_axis=3, concat_axis=1, tiled=True)  23.1 us
    all_to_all x1, blocking collectives, exchange_blocks(): pieces = lax.all_to_all(pieces, axis, split_axis=0, concat_axis=0)  21.7 us
    unnamed x6, local copies, waits for them, and re-layouts  13.1 us
  transfers between devices with their start and end apart: 2, of which 2 were waited for; matrix products, arithmetic and copies ran while one was open for 5% of the time, Pallas kernels for 0%

profile of v1, /device:TPU:0, one launch (start us, length us, event | category | flops | bytes accessed | tf_op | source)
XLA Modules:
  0.0 241.2 jit_solution(17728014064904734612)
XLA Ops:
  6.5 0.0 all-gather.2.cloned.1.call-start
  7.2 2.5 %copy.14 = f32[1,2,160,640]{2,1,0,3:T(2,128)S(1)} copy(f32[1,2,160,640]{3,2,1,0:T(8,128)} %param.6) | data formatting | bytes 1638400 | tf_op args[0]
  9.7 0.8 dynamic_slice.11
  10.5 0.7 dynamic-slice_xor_fusion
  11.2 0.1 broadcast_xor_fusion
  11.3 2.5 %compare_select_fusion = f32[1,2,160,640]{2,1,0,3:T(2,128)S(1)} fusion(f32[1,2,160,640]{2,1,0,3:T(2,128)S(1)} %copy.14, s32[2,160]{1,0:T(2,128)S(1)} %broadcast_xor_fusion, s32[640]{0:T(1024)} %param.11), kind=kLoop, calls=%fused_computation.3 | loop fusion | flops 614400 | bytes 1642240 | tf_op jit(solution)/shard_map/jit(_where)/select_n | solution.py:38
  13.8 23.1 %all_to_all.23 = f32[1,2,160,640]{2,1,0,3:T(2,128)S(1)} all-to-all(f32[1,2,160,640]{2,1,0,3:T(2,128)S(1)} %compare_select_fusion), channel_id=1, replica_groups=mesh['wide'=8,'narrow'=4] {'wide'}, dimensions={3} | all-to-all | bytes 1638400 | tf_op jit(solution)/shard_map/all_to_all | solution.py:39
  36.9 2.2 copy.15
  39.0 0.0 all-gather.2.cloned.1.call-update
  39.1 0.0 reduce-scatter.2.cloned.1.call-start
  39.1 9.9 %copy.17 = f32[16,80,1280]{1,2,0:T(8,128)} copy(f32[16,80,1280]{2,1,0:T(8,128)} %param.7) | data formatting | bytes 13107200 | tf_op args[1]
  49.1 87.6 %all-gather.2.cloned.1.call-done = f32[1,16,640,80]{3,1,0,2:T(8,128)} async-done(((f32[1,16,160,80]{3,1,0,2:T(8,128)}), f32[1,16,640,80]{3,1,0,2:T(8,128)}) %all-gather.2.cloned.1.call-update) | async-done | bytes 3276816 | tf_op jit(solution)/shard_map/all_gather | solution.py:40
  136.7 4.5 %copy.16 = f32[1,16,640,80]{2,3,1,0:T(8,128)S(1)} copy(f32[1,16,640,80]{3,1,0,2:T(8,128)} %all-gather.2.cloned.1.call-done) | data formatting | bytes 6553600 | tf_op jit(solution)/shard_map/all_gather | solution.py:40
  141.1 23.8 %fusion = f32[640,160,8,1]{0,1,3,2:T(8,128)} fusion(f32[16,80,160,8]{1,3,2,0:T(8,128)} %bitcast.34, f32[1,16,640,80]{2,3,1,0:T(8,128)S(1)} %copy.16), kind=kOutput, calls=%fused_computation | convolution fusion | flops 12582912000 | bytes 13107200 | tf_op jit(solution)/shard_map/ikac,kcbj->iajb/dot_general | solution.py:41
  164.9 0.0 copy-start.1
  164.9 0.0 copy-start
  164.9 0.0 reduce-scatter.2.cloned.1.call-update
  165.0 0.6 copy-done.1
  165.6 0.7 dynamic_slice.10
  166.3 0.0 copy-done
  166.3 0.7 xor_xor_fusion
  167.0 43.4 %reduce-scatter.2.cloned.1.call-done = f32[1,640,160]{1,2,0:T(8,128)} async-done(((f32[1,640,1280]{1,2,0:T(8,128)}), f32[1,640,160]{1,2,0:T(8,128)}) %reduce-scatter.2.cloned.1.call-update) | async-done | bytes 409616 | tf_op jit(solution)/shard_map/reduce_scatter | solution.py:43
  210.4 1.1 fusion.3
  211.5 0.2 slice_bitcast_fusion.3
  211.7 21.7 %all_to_all.24 = f32[4,1,160,160]{2,3,1,0:T(8,128)S(1)} all-to-all(f32[4,1,160,160]{2,3,1,0:T(8,128)S(1)} %pad_maximum_fusion), channel_id=1, replica_groups=mesh['wide'=8,'narrow'=4] {'narrow'}, dimensions={0} | all-to-all | bytes 819200 | tf_op jit(solution)/shard_map/all_to_all | solution.py:10
  233.4 1.0 copy.21
  (1 shorter events, 0.0 us)
Async XLA Ops:
  6.5 130.1 %all-gather.2.cloned.1.call-start = ((), (), s32[]{:S(2)}) async-start(), calls=%async_computation.3 | async-start | bytes 6553600 | tf_op jit(solution)/shard_map/all_gather | solution.py:40
  39.1 171.3 %reduce-scatter.2.cloned.1.call-start = ((), (), s32[]{:S(2)}) async-start(), calls=%async_computation.4 | async-start | bytes 3686400 | tf_op jit(solution)/shard_map/reduce_scatter | solution.py:43
  164.9 0.7 copy-start.1
  164.9 1.3 copy-start
Sparse Core Ops, SparseCore 0:
  39.2 97.4 all-gather.1
  165.1 45.2 reduce-scatter.1
